TPU v7x, 256 devices: a whole 4x4x8 slice. The times are simulated.
256 devices in a mesh: fsdp: 64 (over y, z, core), tp: 4 (over x).
Axes of the slice: x: 4, y: 4, z: 8, core: 2. Of those that a mesh axis runs over, the one named last changes fastest.
Arguments:
- grads: float32 [4, 512, 256, 256], P('tp', None, 'fsdp'), may hold values from -200 to 200
- weights: float32 [512, 256, 256], P('tp', 'fsdp'), may hold values from -0.3 to 0.3
- moments: float32 [512, 256, 256], P('tp', 'fsdp'), may hold values from 0.05 to 2
- left_stat: float32 [4, 64, 6, 256, 256], P('tp', 'fsdp'), may hold values from -20 to 200
- right_stat: float32 [4, 64, 6, 256, 256], P('tp', 'fsdp'), may hold values from -20 to 200
- left_root: bfloat16 [4, 64, 6, 256, 256], P('tp', 'fsdp'), may hold values from -1 to 2
- right_root: bfloat16 [4, 64, 6, 256, 256], P('tp', 'fsdp'), may hold values from -1 to 2
- owner: int32 [512], P('tp'), may hold values from 0 to 63, as said below
- extent: int32 [512, 2], P('tp'), may hold values from 1 to 2
Outputs:
- new_weights: float32 [512, 256, 256], P('tp', 'fsdp')
- new_moments: float32 [512, 256, 256], P('tp', 'fsdp')
- new_left: float32 [4, 64, 6, 256, 256], P('tp', 'fsdp')
- new_right: float32 [4, 64, 6, 256, 256], P('tp', 'fsdp')
Inputs may be any that keep to these rules, and one draw needn't show every extreme that they name: `owner`: within each group of 128 consecutive blocks, no device owns more than 6 blocks, and some device owns exactly 6.
All inputs are finite; a program needn't handle non-finite values.
Results may differ from a plain program's by a relative error of at most 0.0003.
Values sent between devices are 32-bit elements; how exact they have to be, the bound alone decides.
A program may use at most 64 MiB of HBM per device.

v0:
```python
import jax
import jax.numpy as jnp
from jax import lax
from jax.sharding import PartitionSpec as P

PRECISE = lax.Precision.HIGHEST
ADAM_BETA = 0.95
STAT_BETA = 0.99
LEARN_RATE = 0.05
ADAM_EPS = 1e-08
NORM_EPS = 1e-06


def extent_mask(extents, row_ids, col_ids, half_size):
    row_live = row_ids[None, :] < extents[:, 0:1] * half_size
    col_live = col_ids[None, :] < extents[:, 1:2] * half_size
    return (row_live[:, :, None] & col_live[:, None, :]).astype(jnp.float32)


def slot_tables(owner_col, owners, load_max):
    column = owner_col.shape[0]
    onehot = (owner_col[:, None] == jnp.arange(owners, dtype=jnp.int32)[None, :]).astype(jnp.int32)
    slot_rank = jnp.sum((jnp.cumsum(onehot, axis=0) - onehot) * onehot, axis=1)
    flat_slot = owner_col * load_max + slot_rank
    slot_hits = flat_slot[:, None] == jnp.arange(owners * load_max, dtype=jnp.int32)[None, :]
    valid_slot = jnp.any(slot_hits, axis=0)
    block_index = jnp.sum(
        jnp.where(slot_hits, jnp.arange(column, dtype=jnp.int32)[:, None], 0), axis=0
    )
    return (flat_slot, valid_slot, block_index)


def refresh(slot_grad, left_old, right_old, left_inv, right_inv, slot_mask):
    left_prod = jnp.einsum("sij,skj->sik", slot_grad, slot_grad, precision=PRECISE)
    right_prod = jnp.einsum("sji,sjk->sik", slot_grad, slot_grad, precision=PRECISE)
    left_new = STAT_BETA * left_old + (1.0 - STAT_BETA) * left_prod
    right_new = STAT_BETA * right_old + (1.0 - STAT_BETA) * right_prod
    inner = jnp.einsum("sij,sjk->sik", left_inv.astype(jnp.float32), slot_grad, precision=PRECISE)
    precond = (
        jnp.einsum("sij,sjk->sik", inner, right_inv.astype(jnp.float32), precision=PRECISE)
        * slot_mask
    )
    return (left_new, right_new, precond)


def on_device(grads, weights, moments, left_stat, right_stat, left_root, right_root, owner, extent):
    owners = lax.axis_size("fsdp")
    my_index = lax.axis_index("fsdp")
    count_blocks, shard_rows, block_size = weights.shape
    load_max = left_stat.shape[2]
    half_size = block_size // 2
    summed = lax.psum_scatter(grads[0], "tp", scatter_dimension=0, tiled=True)
    row_ids = my_index * shard_rows + jnp.arange(shard_rows, dtype=jnp.int32)
    col_ids = jnp.arange(block_size, dtype=jnp.int32)
    summed = summed * extent_mask(extent, row_ids, col_ids, half_size)
    new_moment = ADAM_BETA * moments + (1.0 - ADAM_BETA) * summed * summed
    adam_dir = summed / (jnp.sqrt(new_moment) + ADAM_EPS)
    adam_part = jnp.sum(adam_dir * adam_dir, axis=(1, 2))
    flat_slot, valid_slot, block_index = slot_tables(owner, owners, load_max)
    adam_total = lax.psum(adam_part, "fsdp")
    outgoing = jnp.take(summed, block_index, axis=0) * valid_slot[:, None, None].astype(jnp.float32)
    outgoing = outgoing.reshape(owners, load_max, shard_rows, block_size)
    incoming = lax.all_to_all(outgoing, "fsdp", split_axis=0, concat_axis=2, tiled=True)[0]
    mine_index = lax.dynamic_slice_in_dim(block_index, my_index * load_max, load_max)
    mine_extent = jnp.take(extent, mine_index, axis=0)
    out_mask = extent_mask(mine_extent, col_ids, col_ids, half_size)
    left_new, right_new, precond = refresh(
        incoming, left_stat[0, 0], right_stat[0, 0], left_root[0, 0], right_root[0, 0], out_mask
    )
    prec_owner = jnp.sum(precond * precond, axis=(1, 2))
    spread_sq = jnp.broadcast_to(prec_owner[None, :, None], (1, load_max, owners))
    back_prec, back_sq = (
        lax.all_to_all(precond[None], "fsdp", split_axis=2, concat_axis=0, tiled=True),
        lax.all_to_all(spread_sq, "fsdp", split_axis=2, concat_axis=0, tiled=True),
    )
    home_prec = jnp.take(
        back_prec.reshape(owners * load_max, shard_rows, block_size), flat_slot, axis=0
    )
    prec_total = jnp.take(back_sq.reshape(owners * load_max), flat_slot)
    graft = jnp.sqrt(adam_total / (prec_total + NORM_EPS))
    new_weight = weights - LEARN_RATE * home_prec * graft[:, None, None]
    return (new_weight, new_moment, left_new[None, None], right_new[None, None])


def solution(mesh):
    in_specs = (
        P("tp", None, "fsdp", None),
        P("tp", "fsdp", None),
        P("tp", "fsdp", None),
        P("tp", "fsdp", None, None, None),
        P("tp", "fsdp", None, None, None),
        P("tp", "fsdp", None, None, None),
        P("tp", "fsdp", None, None, None),
        P("tp"),
        P("tp", None),
    )
    out_specs = (
        P("tp", "fsdp", None),
        P("tp", "fsdp", None),
        P("tp", "fsdp", None, None, None),
        P("tp", "fsdp", None, None, None),
    )
    return jax.shard_map(
        on_device, mesh=mesh, in_specs=in_specs, out_specs=out_specs, check_vma=False
    )
```

profile of v0, /device:TPU:1, one launch (start us, length us, event | category | flops | bytes accessed | tf_op | source)
XLA Modules:
  0.0 339.6 jit_solution(3484285128444985306)
XLA Ops:
  7.3 0.7 all-reduce.3.cloned.1.call-update
  8.1 0.2 reduce_window_sum.11
  8.2 0.2 select_reduce_fusion.1
  8.6 0.1 reshape.161
  8.8 0.1 reduce_sum.42
  9.0 0.6 dynamic-slice
  10.5 67.6 %all-reduce.3.cloned.1.call-done = f32[512,4,256]{2,1,0:T(4,128)} async-done(((f32[512,4,256]{2,1,0:T(4,128)}), f32[512,4,256]{2,1,0:T(4,128)}) %all-reduce.3.cloned.1.call-update) | async-done | bytes 2097168
  78.0 3.7 %multiply_reduce_fusion.1 = (f32[128]{0:T(128)S(1)}, f32[128,4,256]{2,1,0:T(4,128)}, f32[128,4,256]{2,1,0:T(4,128)S(1)}) fusion(f32[128,4,256]{2,1,0:T(4,128)S(1)} %copy-done.3, f32[512,4,256]{2,1,0:T(4,128)} %all-reduce.3.cloned.1.call-done, u32[]{:T(128)S(6)} %multiply.3, pred[128,256]{1,0:T(8,128)(4,1)S(1)} %iota_compare_fusion.1, ...), kind=kLoop, calls=%fused_computation.18 | loop fusion | flops 1310592 | bytes 2130948 | tf_op jit(solution)/shard_map/reduce_sum | solution.py:58
  81.7 2.5 gather_fusion.1
  84.2 2.3 select_multiply_fusion
  86.5 10.7 %all-to-all-start = ((f32[64,6,4,256]{3,2,1,0:T(4,128)}), f32[64,6,4,256]{3,2,1,0:T(4,128)S(1)}, u32[]{:S(2)}, u32[]{:S(2)}) async-start(f32[64,6,4,256]{3,2,1,0:T(4,128)} %select_multiply_fusion), calls=%async_computation | async-start | bytes 3145728 | tf_op jit(solution)/shard_map/all_to_all | solution.py:63
  97.4 0.6 gather_fusion
  98.0 0.2 multiply_reduce_fusion.3
  98.3 38.7 %all-to-all-done = f32[64,6,4,256]{3,2,1,0:T(4,128)S(1)} async-done(((f32[64,6,4,256]{3,2,1,0:T(4,128)}), f32[64,6,4,256]{3,2,1,0:T(4,128)S(1)}, u32[]{:S(2)}, u32[]{:S(2)}) %all-to-all-start) | async-done | bytes 1572896 | tf_op jit(solution)/shard_map/all_to_all | solution.py:63
  137.0 1.4 copy.53
  138.4 1.9 squeeze.15
  140.3 1.0 fusion.3
  141.3 2.3 multiply_reduce_fusion
  143.6 0.6 broadcast_in_dim.88
  144.2 6.1 %all-to-all-start.2 = ((f32[1,6,64]{1,0,2:T(1,128)}), f32[1,6,64]{1,0,2:T(1,128)S(1)}, u32[]{:S(2)}, u32[]{:S(2)}) async-start(f32[1,6,64]{1,0,2:T(1,128)} %broadcast_in_dim.88), calls=%async_computation.2 | async-start | bytes 65536 | tf_op jit(solution)/shard_map/all_to_all | solution.py:74
  150.3 4.2 %copy.56 = f32[1,6,256,256]{3,0,1,2:T(1,128)} copy(f32[1,6,256,256]{3,2,1,0:T(8,128)} %bitcast.49) | data formatting | bytes 3145728 | tf_op jit(solution)/shard_map/broadcast_in_dim | solution.py:73
  154.5 5.0 %all-to-all-done.2 = f32[1,6,64]{1,0,2:T(1,128)S(1)} async-done(((f32[1,6,64]{1,0,2:T(1,128)}), f32[1,6,64]{1,0,2:T(1,128)S(1)}, u32[]{:S(2)}, u32[]{:S(2)}) %all-to-all-start.2) | async-done | bytes 1568 | tf_op jit(solution)/shard_map/all_to_all | solution.py:74
  159.5 5.5 %all-to-all-start.1 = ((f32[1,6,256,256]{3,0,1,2:T(1,128)}), f32[1,6,256,256]{3,0,1,2:T(1,128)}, u32[]{:S(2)}, u32[]{:S(2)}) async-start(f32[1,6,256,256]{3,0,1,2:T(1,128)} %copy.56), calls=%async_computation.1 | async-start | bytes 3145728 | tf_op jit(solution)/shard_map/all_to_all | solution.py:73
  165.1 152.9 %psum.7 = f32[128]{0:T(128)S(1)} all-reduce(f32[128]{0:T(128)S(1)} %get-tuple-element.8), channel_id=1, replica_groups=mesh['fsdp'=64,'tp'=4] {'fsdp'}, use_global_device_ids=true, to_apply=%region_6.7 | all-reduce | flops 128 | bytes 1024 | tf_op jit(solution)/shard_map/psum | solution.py:60
  318.0 4.5 %fusion.1 = f32[1,1,6,256,256]{4,3,2,1,0:T(8,128)} fusion(f32[1,1,6,256,256]{4,3,2,1,0:T(8,128)} %param.12, f32[6,256,256]{2,1,0:T(8,128)S(1)} %squeeze.15), kind=kOutput, calls=%fused_computation.7 | convolution fusion | flops 1209139200 | bytes 4718592 | tf_op jit(solution)/shard_map/sij,skj->sik/dot_general | solution.py:34
  322.5 3.9 %fusion = f32[1,1,6,256,256]{4,3,2,1,0:T(8,128)} fusion(f32[1,1,6,256,256]{4,3,2,1,0:T(8,128)S(1)} %copy-done.1, f32[6,256,256]{2,1,0:T(8,128)S(1)} %squeeze.15), kind=kOutput, calls=%fused_computation.5 | convolution fusion | flops 1209139200 | bytes 4718592 | tf_op jit(solution)/shard_map/sji,sjk->sik/dot_general | solution.py:35
  326.4 0.1 reshape.160
  326.5 1.3 gather_fusion.3
  327.8 2.5 copy.57
  330.3 0.4 copy.58
  330.8 0.9 gather_fusion.2
  331.7 1.1 multiply_subtract_fusion
  (37 shorter events, 1.0 us)
Async XLA Ops:
  7.2 134.1 %copy-start = (bf16[1,1,6,256,256]{4,3,2,1,0:T(8,128)(2,1)S(1)}, bf16[1,1,6,256,256]{4,3,2,1,0:T(8,128)(2,1)}, u32[]{:S(2)}) copy-start(bf16[1,1,6,256,256]{4,3,2,1,0:T(8,128)(2,1)} %param.15) | copy-start | bytes 2359300
  7.2 1.8 copy-start.7
  7.2 0.8 copy-start.5
  7.2 3.0 copy-start.6
  7.2 70.8 %copy-start.3 = (f32[128,4,256]{2,1,0:T(4,128)S(1)}, f32[128,4,256]{2,1,0:T(4,128)}, u32[]{:S(2)}) copy-start(f32[128,4,256]{2,1,0:T(4,128)} %param.11) | copy-start | bytes 1572868
  7.2 70.8 %all-reduce.3.cloned.1.call-start = ((), (), s32[]{:S(2)}) async-start(), calls=%async_computation.3 | async-start | bytes 4194304
  86.5 50.5 %all-to-all-start = ((f32[64,6,4,256]{3,2,1,0:T(4,128)}), f32[64,6,4,256]{3,2,1,0:T(4,128)S(1)}, u32[]{:S(2)}, u32[]{:S(2)}) async-start(f32[64,6,4,256]{3,2,1,0:T(4,128)} %select_multiply_fusion), calls=%async_computation | async-start | bytes 3145728 | tf_op jit(solution)/shard_map/all_to_all | solution.py:63
  138.4 1.9 copy-start.2
  144.2 15.3 %all-to-all-start.2 = ((f32[1,6,64]{1,0,2:T(1,128)}), f32[1,6,64]{1,0,2:T(1,128)S(1)}, u32[]{:S(2)}, u32[]{:S(2)}) async-start(f32[1,6,64]{1,0,2:T(1,128)} %broadcast_in_dim.88), calls=%async_computation.2 | async-start | bytes 65536 | tf_op jit(solution)/shard_map/all_to_all | solution.py:74
  159.5 168.3 %all-to-all-start.1 = ((f32[1,6,256,256]{3,0,1,2:T(1,128)}), f32[1,6,256,256]{3,0,1,2:T(1,128)}, u32[]{:S(2)}, u32[]{:S(2)}) async-start(f32[1,6,256,256]{3,0,1,2:T(1,128)} %copy.56), calls=%async_computation.1 | async-start | bytes 3145728 | tf_op jit(solution)/shard_map/all_to_all | solution.py:73
  318.0 4.5 %copy-start.1 = (f32[1,1,6,256,256]{4,3,2,1,0:T(8,128)S(1)}, f32[1,1,6,256,256]{4,3,2,1,0:T(8,128)}, u32[]{:S(2)}) copy-start(f32[1,1,6,256,256]{4,3,2,1,0:T(8,128)} %param.13) | copy-start | bytes 4718596
  330.3 1.3 copy-start.4
Sparse Core Ops, SparseCore 0:
  10.4 67.5 all-reduce.2
where the time goes:
time: 340 us
  blocking collectives  153 us (45%)
  waiting for transfers between devices  112 us (33%)
  starting transfers between devices  22.4 us (7%)
  local copies, waits for them, and re-layouts  17.3 us (5%)
  between operations  15 us (4%)
  matrix products  11.6 us (3%)
  other arithmetic  8.41 us (2%)
    psum x1, blocking collectives, on_device(): adam_total = lax.psum(adam_part, 'fsdp')  153 us
    unnamed x2, waiting for transfers between devices  68.2 us
    all_to_all x1, waiting for transfers between devices, on_device(): lax.all_to_all(outgoing, 'fsdp', split_axis=0, concat_axis=2, tiled=True)[0]  38.7 us
    all_to_all x1, starting transfers between devices, on_device(): lax.all_to_all(outgoing, 'fsdp', split_axis=0, concat_axis=2, tiled=True)[0]  10.7 us
  transfers between devices with their start and end apart: 4, of which 3 were waited for; matrix products, arithmetic and copies ran while one was open for 5% of the time, Pallas kernels for 0%

commit v1 on v0

--- a/solution.py
+++ b/solution.py
@@ -57,7 +57,7 @@
     adam_dir = summed / (jnp.sqrt(new_moment) + ADAM_EPS)
     adam_part = jnp.sum(adam_dir * adam_dir, axis=(1, 2))
     flat_slot, valid_slot, block_index = slot_tables(owner, owners, load_max)
-    adam_total = lax.psum(adam_part, "fsdp")
+    adam_total = jnp.sum(lax.all_gather(adam_part, "fsdp"), axis=0)
     outgoing = jnp.take(summed, block_index, axis=0) * valid_slot[:, None, None].astype(jnp.float32)
     outgoing = outgoing.reshape(owners, load_max, shard_rows, block_size)
     incoming = lax.all_to_all(outgoing, "fsdp", split_axis=0, concat_axis=2, tiled=True)[0]

time: 340 us -> 258 us (0.76)
  blocking collectives: 153 us -> 70.6 us
    psum x1 -> x0, blocking collectives: 153 us -> none  [on_device(): adam_total = lax.psum(adam_part, 'fsdp')]
    all_gather x0 -> x1, blocking collectives: none -> 70.6 us  [on_device(): adam_total = jnp.sum(lax.all_gather(adam_part, 'fsdp'), axis=0)]
  transfers between devices with their start and end apart: 4 -> 4, of which waited for: 3 -> 3; matrix products, arithmetic and copies ran while one was open for 5% -> 7% of each run, Pallas kernels for 0% -> 0%
where the time goes in v1:
time: 258 us; the launch traced here: 257 us
  waiting for transfers between devices  112 us (43%)
  blocking collectives  70.6 us (27%)
  starting transfers between devices  22.4 us (9%)
  local copies, waits for them, and re-layouts  17.3 us (7%)
  between operations  15 us (6%)
  matrix products  11.6 us (4%)
  other arithmetic  8.5 us (3%)
    all_gather x1, blocking collectives, on_device(): adam_total = jnp.sum(lax.all_gather(adam_part, 'fsdp'), axis=0)  70.6 us
    unnamed x2, waiting for transfers between devices  68.2 us
    all_to_all x1, waiting for transfers between devices, on_device(): lax.all_to_all(outgoing, 'fsdp', split_axis=0, concat_axis=2, tiled=True)[0]  38.7 us
    all_to_all x1, starting transfers between devices, on_device(): lax.all_to_all(outgoing, 'fsdp', split_axis=0, concat_axis=2, tiled=True)[0]  10.7 us
    all_to_all x1, starting transfers between devices, on_device(): lax.all_to_all(spread_sq, 'fsdp', split_axis=2, concat_axis=0, tiled=True)  6.12 us
    all_to_all x1, starting transfers between devices, on_device(): lax.all_to_all(precond[None], 'fsdp', split_axis=2, concat_axis=0, tiled=...  5.53 us
  transfers between devices with their start and end apart: 4, of which 3 were waited for; matrix products, arithmetic and copies ran while one was open for 7% of the time, Pallas kernels for 0%

profile of v1, /device:TPU:1, one launch (start us, length us, event | category | flops | bytes accessed | tf_op | source)
XLA Modules:
  0.0 257.4 jit_solution(16045657726888296485)
XLA Ops:
  7.3 0.7 all-reduce.3.cloned.1.call-update
  8.1 0.2 reduce_window_sum.11
  8.2 0.2 select_reduce_fusion.1
  8.6 0.1 reshape.169
  8.8 0.1 reduce_sum.51
  9.0 0.6 dynamic-slice
  10.5 67.6 %all-reduce.3.cloned.1.call-done = f32[512,4,256]{2,1,0:T(4,128)} async-done(((f32[512,4,256]{2,1,0:T(4,128)}), f32[512,4,256]{2,1,0:T(4,128)}) %all-reduce.3.cloned.1.call-update) | async-done | bytes 2097168
  78.0 3.7 %multiply_reduce_fusion.1 = (f32[128]{0:T(128)S(1)}, f32[128,4,256]{2,1,0:T(4,128)}, f32[128,4,256]{2,1,0:T(4,128)S(1)}) fusion(f32[128,4,256]{2,1,0:T(4,128)S(1)} %copy-done.3, f32[512,4,256]{2,1,0:T(4,128)} %all-reduce.3.cloned.1.call-done, u32[]{:T(128)S(6)} %multiply.3, pred[128,256]{1,0:T(8,128)(4,1)S(1)} %iota_compare_fusion.1, ...), kind=kLoop, calls=%fused_computation.18 | loop fusion | flops 1310592 | bytes 2130948 | tf_op jit(solution)/shard_map/reduce_sum | solution.py:58
  81.7 2.5 gather_fusion.1
  84.2 2.3 select_multiply_fusion
  86.5 10.7 %all-to-all-start = ((f32[64,6,4,256]{3,2,1,0:T(4,128)}), f32[64,6,4,256]{3,2,1,0:T(4,128)S(1)}, u32[]{:S(2)}, u32[]{:S(2)}) async-start(f32[64,6,4,256]{3,2,1,0:T(4,128)} %select_multiply_fusion), calls=%async_computation | async-start | bytes 3145728 | tf_op jit(solution)/shard_map/all_to_all | solution.py:63
  97.4 0.6 gather_fusion
  98.0 0.2 multiply_reduce_fusion.3
  98.3 38.7 %all-to-all-done = f32[64,6,4,256]{3,2,1,0:T(4,128)S(1)} async-done(((f32[64,6,4,256]{3,2,1,0:T(4,128)}), f32[64,6,4,256]{3,2,1,0:T(4,128)S(1)}, u32[]{:S(2)}, u32[]{:S(2)}) %all-to-all-start) | async-done | bytes 1572896 | tf_op jit(solution)/shard_map/all_to_all | solution.py:63
  137.0 1.4 copy.53
  138.4 1.9 squeeze.15
  140.3 1.0 fusion.3
  141.3 2.3 multiply_reduce_fusion
  143.6 0.6 broadcast_in_dim.88
  144.2 6.1 %all-to-all-start.2 = ((f32[1,6,64]{1,0,2:T(1,128)}), f32[1,6,64]{1,0,2:T(1,128)S(1)}, u32[]{:S(2)}, u32[]{:S(2)}) async-start(f32[1,6,64]{1,0,2:T(1,128)} %broadcast_in_dim.88), calls=%async_computation.2 | async-start | bytes 65536 | tf_op jit(solution)/shard_map/all_to_all | solution.py:74
  150.3 4.2 %copy.56 = f32[1,6,256,256]{3,0,1,2:T(1,128)} copy(f32[1,6,256,256]{3,2,1,0:T(8,128)} %bitcast.50) | data formatting | bytes 3145728 | tf_op jit(solution)/shard_map/broadcast_in_dim | solution.py:73
  154.5 5.0 %all-to-all-done.2 = f32[1,6,64]{1,0,2:T(1,128)S(1)} async-done(((f32[1,6,64]{1,0,2:T(1,128)}), f32[1,6,64]{1,0,2:T(1,128)S(1)}, u32[]{:S(2)}, u32[]{:S(2)}) %all-to-all-start.2) | async-done | bytes 1568 | tf_op jit(solution)/shard_map/all_to_all | solution.py:74
  159.5 5.5 %all-to-all-start.1 = ((f32[1,6,256,256]{3,0,1,2:T(1,128)}), f32[1,6,256,256]{3,0,1,2:T(1,128)}, u32[]{:S(2)}, u32[]{:S(2)}) async-start(f32[1,6,256,256]{3,0,1,2:T(1,128)} %copy.56), calls=%async_computation.1 | async-start | bytes 3145728 | tf_op jit(solution)/shard_map/all_to_all | solution.py:73
  165.1 70.6 %all-gather.1 = f32[64,1,128]{2,1,0:T(1,128)S(1)} all-gather(f32[1,1,128]{2,1,0:T(1,128)S(1)} %bitcast.56), channel_id=2, replica_groups=mesh['fsdp'=64,'tp'=4] {'fsdp'}, dimensions={0}, use_global_device_ids=true | all-gather | bytes 33280 | tf_op jit(solution)/shard_map/all_gather | solution.py:60
  235.8 4.5 %fusion.1 = f32[1,1,6,256,256]{4,3,2,1,0:T(8,128)} fusion(f32[1,1,6,256,256]{4,3,2,1,0:T(8,128)} %param.12, f32[6,256,256]{2,1,0:T(8,128)S(1)} %squeeze.15), kind=kOutput, calls=%fused_computation.7 | convolution fusion | flops 1209139200 | bytes 4718592 | tf_op jit(solution)/shard_map/sij,skj->sik/dot_general | solution.py:34
  240.2 3.9 %fusion = f32[1,1,6,256,256]{4,3,2,1,0:T(8,128)} fusion(f32[1,1,6,256,256]{4,3,2,1,0:T(8,128)S(1)} %copy-done.1, f32[6,256,256]{2,1,0:T(8,128)S(1)} %squeeze.15), kind=kOutput, calls=%fused_computation.5 | convolution fusion | flops 1209139200 | bytes 4718592 | tf_op jit(solution)/shard_map/sji,sjk->sik/dot_general | solution.py:35
  244.1 0.1 reshape.168
  244.3 1.3 gather_fusion.3
  245.6 2.5 copy.57
  248.1 0.4 copy.58
  248.5 0.9 gather_fusion.2
  249.4 1.1 multiply_subtract_fusion
  (38 shorter events, 1.1 us)
Async XLA Ops:
  7.2 134.1 %copy-start = (bf16[1,1,6,256,256]{4,3,2,1,0:T(8,128)(2,1)S(1)}, bf16[1,1,6,256,256]{4,3,2,1,0:T(8,128)(2,1)}, u32[]{:S(2)}) copy-start(bf16[1,1,6,256,256]{4,3,2,1,0:T(8,128)(2,1)} %param.15) | copy-start | bytes 2359300
  7.2 1.8 copy-start.7
  7.2 0.8 copy-start.5
  7.2 3.0 %copy-start.6 = (s32[128,2]{0,1:T(2,128)S(1)}, s32[128,2]{0,1:T(2,128)}, u32[]{:S(2)}) copy-start(s32[128,2]{0,1:T(2,128)} %param.17) | copy-start | bytes 3076
  7.2 70.8 %copy-start.3 = (f32[128,4,256]{2,1,0:T(4,128)S(1)}, f32[128,4,256]{2,1,0:T(4,128)}, u32[]{:S(2)}) copy-start(f32[128,4,256]{2,1,0:T(4,128)} %param.11) | copy-start | bytes 1572868
  7.2 70.8 %all-reduce.3.cloned.1.call-start = ((), (), s32[]{:S(2)}) async-start(), calls=%async_computation.3 | async-start | bytes 4194304
  86.5 50.5 %all-to-all-start = ((f32[64,6,4,256]{3,2,1,0:T(4,128)}), f32[64,6,4,256]{3,2,1,0:T(4,128)S(1)}, u32[]{:S(2)}, u32[]{:S(2)}) async-start(f32[64,6,4,256]{3,2,1,0:T(4,128)} %select_multiply_fusion), calls=%async_computation | async-start | bytes 3145728 | tf_op jit(solution)/shard_map/all_to_all | solution.py:63
  138.4 1.9 copy-start.2
  144.2 15.3 %all-to-all-start.2 = ((f32[1,6,64]{1,0,2:T(1,128)}), f32[1,6,64]{1,0,2:T(1,128)S(1)}, u32[]{:S(2)}, u32[]{:S(2)}) async-start(f32[1,6,64]{1,0,2:T(1,128)} %broadcast_in_dim.88), calls=%async_computation.2 | async-start | bytes 65536 | tf_op jit(solution)/shard_map/all_to_all | solution.py:74
  159.5 86.0 %all-to-all-start.1 = ((f32[1,6,256,256]{3,0,1,2:T(1,128)}), f32[1,6,256,256]{3,0,1,2:T(1,128)}, u32[]{:S(2)}, u32[]{:S(2)}) async-start(f32[1,6,256,256]{3,0,1,2:T(1,128)} %copy.56), calls=%async_computation.1 | async-start | bytes 3145728 | tf_op jit(solution)/shard_map/all_to_all | solution.py:73
  235.8 4.5 %copy-start.1 = (f32[1,1,6,256,256]{4,3,2,1,0:T(8,128)S(1)}, f32[1,1,6,256,256]{4,3,2,1,0:T(8,128)}, u32[]{:S(2)}) copy-start(f32[1,1,6,256,256]{4,3,2,1,0:T(8,128)} %param.13) | copy-start | bytes 4718596
  248.1 1.3 copy-start.4
Sparse Core Ops, SparseCore 0:
  10.4 67.5 all-reduce.2
